TPU v7x, 512 devices: a whole 4x4x16 slice. The times are simulated.
512 devices in a mesh: depth: 32 (over x, y, core), strip: 16 (over z).
Axes of the slice: x: 4, y: 4, z: 16, core: 2. Of those that a mesh axis runs over, the one named last changes fastest.
Arguments:
- density: float32 [128, 256, 2048], P('depth', 'strip'), may hold values from -6 to 6
- materials: int32 [128, 256, 2048], P('depth', 'strip'), may hold values from 0 to 3
- occupancy_flags: int32 [32, 16, 16], P('depth', 'strip'), may hold values from 0 to 1, as said below
- tf_color: float32 [4, 3, 16], replicated, may hold values from 0.1 to 1
- tf_opacity: float32 [4, 16], replicated, may hold values from 0.0005 to 0.05
Outputs:
- image: float32 [4, 256, 2048], P(None, 'strip', 'depth')
Inputs may be any that keep to these rules, and one draw needn't show every extreme that they name: `occupancy_flags`: occupied tiles cluster around one depth slab drawn from the seed; the share of occupied tiles differs strongly between depth slabs.
All inputs are finite; a program needn't handle non-finite values.
Results may differ from a plain program's by a relative error of at most 0.0003.
Values sent between devices are 32-bit elements; how exact they have to be, the bound alone decides.
A program may use at most 64 MiB of HBM per device.

v0:
```python
import jax
import jax.numpy as jnp
from jax import lax
from jax.sharding import PartitionSpec as P

light_x = 1.0 / 3.0
light_y = 2.0 / 3.0
light_z = 2.0 / 3.0
ambient = 0.3
diffuse = 0.7


def with_halo(array, sides, width):
    for axis, dim in sides:
        devices, length = (lax.axis_size(axis), array.shape[dim])
        up = [(i, (i + 1) % devices) for i in range(devices - 1)]
        down = [(j, i) for i, j in up]
        last = lax.slice_in_dim(array, length - width, length, axis=dim)
        first = lax.slice_in_dim(array, 0, width, axis=dim)
        before = lax.ppermute(last, axis, up)
        after = lax.ppermute(first, axis, down)
        array = jnp.concatenate([before, array, after], axis=dim)
    return array


def shade_slice(before, here, after, material_slice, occupied, knot_table):
    sample = here[1:-1, 1:-1]
    grad_z = 0.5 * (after[1:-1, 1:-1] - before[1:-1, 1:-1])
    grad_y = 0.5 * (here[2:, 1:-1] - here[:-2, 1:-1])
    grad_x = 0.5 * (here[1:-1, 2:] - here[1:-1, :-2])
    knot_count = knot_table.shape[1]
    material_count = knot_table.shape[0] // 4
    position = jnp.clip(
        (sample.reshape(-1) + 3.0) * ((knot_count - 1) / 6.0), 0.0, knot_count - 1.0
    )
    knot_grid = jnp.arange(knot_count, dtype=jnp.float32)[:, None]
    tent_weights = jnp.maximum(0.0, 1.0 - jnp.abs(position[None, :] - knot_grid))
    looked = jnp.dot(
        knot_table,
        tent_weights,
        precision=lax.Precision.HIGHEST,
        preferred_element_type=jnp.float32,
    )
    onehot = (
        material_slice.reshape(-1)[None, :] == jnp.arange(material_count, dtype=jnp.int32)[:, None]
    ).astype(jnp.float32)
    colour = jnp.sum(
        looked[: 3 * material_count].reshape(material_count, 3, -1) * onehot[:, None, :], axis=0
    )
    density_rate = jnp.sum(looked[3 * material_count :] * onehot, axis=0) * occupied.reshape(-1)
    facing = (grad_x * light_x + grad_y * light_y + grad_z * light_z).reshape(-1)
    steepness = (grad_x * grad_x + grad_y * grad_y + grad_z * grad_z).reshape(-1)
    lighting = ambient + diffuse * jnp.abs(facing) / jnp.sqrt(1.0 + steepness)
    opacity_step = 1.0 - jnp.exp(-density_rate)
    return (colour * (lighting * opacity_step)[None, :], opacity_step)


def composite_over(nearer, farther):
    return jnp.concatenate(
        [nearer[:3] + nearer[3:] * farther[:3], nearer[3:] * farther[3:]], axis=0
    )


def on_device(density, materials, occupancy_flags, tf_color, tf_opacity):
    slab_depth, row_count, columns = density.shape
    material_count = tf_color.shape[0]
    knot_count = tf_color.shape[2]
    knot_table = jnp.concatenate(
        [tf_color.reshape(material_count * 3, knot_count), tf_opacity], axis=0
    )
    padded = with_halo(density, (("depth", 0), ("strip", 1)), 1)
    padded = jnp.pad(padded, ((0, 0), (0, 0), (1, 1)))
    tile_count = occupancy_flags.shape[2]
    tile_row = jnp.repeat(occupancy_flags[0, 0], columns // tile_count).astype(jnp.float32)
    occupied = jnp.broadcast_to(tile_row[None, :], (row_count, columns))

    def advance(state_carry, slab_index):
        radiance, transmit = state_carry
        before = lax.dynamic_index_in_dim(padded, slab_index, 0, keepdims=False)
        here = lax.dynamic_index_in_dim(padded, slab_index + 1, 0, keepdims=False)
        after = lax.dynamic_index_in_dim(padded, slab_index + 2, 0, keepdims=False)
        material_slice = lax.dynamic_index_in_dim(materials, slab_index, 0, keepdims=False)
        emitted, opacity_step = shade_slice(
            before, here, after, material_slice, occupied, knot_table
        )
        return ((radiance + transmit[None, :] * emitted, transmit * (1.0 - opacity_step)), None)

    start = (
        jnp.zeros((3, row_count * columns), jnp.float32),
        jnp.ones((row_count * columns,), jnp.float32),
    )
    (radiance, transmit), _ = lax.scan(advance, start, jnp.arange(slab_depth, dtype=jnp.int32))
    partial_value = jnp.concatenate([radiance, transmit[None, :]], axis=0).reshape(
        4, row_count, columns
    )
    groups = lax.axis_size("depth")
    levels = groups.bit_length() - 1
    block_width = columns // groups
    pieces = lax.all_to_all(partial_value, "depth", split_axis=2, concat_axis=1, tiled=True)
    pieces = pieces.reshape(4, groups, row_count, block_width)
    for section_bit in range(levels):
        pieces = composite_over(pieces[:, 0::2], pieces[:, 1::2])
    finished = pieces[:, 0]
    return jnp.concatenate([finished[:3], 1.0 - finished[3:]], axis=0)


def solution(mesh):
    placed = (
        P("depth", "strip", None),
        P("depth", "strip", None),
        P("depth", "strip", None),
        P(),
        P(),
    )
    return jax.shard_map(
        on_device, mesh=mesh, in_specs=placed, out_specs=P(None, "strip", "depth"), check_vma=False
    )
```

profile of v0, /device:TPU:225, one launch (start us, length us, event | category | flops | bytes accessed | tf_op | source)
XLA Modules:
  0.0 129.5 jit_solution(18345752158085729972)
XLA Ops:
  0.0 1.0 fusion.26
  1.0 2.6 %collective-permute-start.1 = (f32[1,16,2048]{2,1,0:T(8,128)S(1)}, f32[1,16,2048]{2,1,0:T(8,128)S(1)}, u32[]{:S(2)}, u32[]{:S(2)}) collective-permute-start(f32[1,16,2048]{2,1,0:T(8,128)S(1)} %get-tuple-element.198), channel_id=1, source_target_pairs={{16,0},{32,16},{48,32},{64,48},{80,64},{96,80},{112,96},{128,112},... | collective-permute-start | bytes 393224 | tf_op jit(solution)/shard_map/ppermute | solution.py:21
  3.6 3.1 %collective-permute-start = (f32[1,16,2048]{2,1,0:T(8,128)S(1)}, f32[1,16,2048]{2,1,0:T(8,128)S(1)}, u32[]{:S(2)}, u32[]{:S(2)}) collective-permute-start(f32[1,16,2048]{2,1,0:T(8,128)S(1)} %get-tuple-element.199), channel_id=1, source_target_pairs={{0,16},{16,32},{32,48},{48,64},{64,80},{80,96},{96,112},{112,128},... | collective-permute-start | bytes 393224 | tf_op jit(solution)/shard_map/ppermute | solution.py:20
  7.4 0.7 copy.10
  8.6 1.1 constant_dynamic-update-slice_fusion.1
  9.8 4.8 %collective-permute-start.2 = (f32[6,1,2048]{2,1,0:T(1,128)S(1)}, f32[6,1,2048]{2,1,0:T(1,128)S(1)}, u32[]{:S(2)}, u32[]{:S(2)}) collective-permute-start(f32[6,1,2048]{2,1,0:T(1,128)S(1)} %get-tuple-element.194), channel_id=1, source_target_pairs={{0,1},{1,2},{2,3},{3,4},{4,5},{5,6},{6,7},{7,8},{8,9},{9,10},{10,1... | collective-permute-start | bytes 147464 | tf_op jit(solution)/shard_map/ppermute | solution.py:20
  14.6 1.9 %collective-permute-start.3 = (f32[6,1,2048]{2,1,0:T(1,128)S(1)}, f32[6,1,2048]{2,1,0:T(1,128)S(1)}, u32[]{:S(2)}, u32[]{:S(2)}) collective-permute-start(f32[6,1,2048]{2,1,0:T(1,128)S(1)} %get-tuple-element.195), channel_id=1, source_target_pairs={{1,0},{2,1},{3,2},{4,3},{5,4},{6,5},{7,6},{8,7},{9,8},{10,9},{11,1... | collective-permute-start | bytes 147464 | tf_op jit(solution)/shard_map/ppermute | solution.py:21
  16.6 4.2 %collective-permute-done.3 = f32[6,1,2048]{2,1,0:T(1,128)S(1)} collective-permute-done((f32[6,1,2048]{2,1,0:T(1,128)S(1)}, f32[6,1,2048]{2,1,0:T(1,128)S(1)}, u32[]{:S(2)}, u32[]{:S(2)}) %collective-permute-start.3) | collective-permute-done | bytes 49184 | tf_op jit(solution)/shard_map/ppermute | solution.py:21
  21.4 63.1 %while.16 = (s32[]{:T(128)}, f32[3,32768]{1,0:T(4,128)S(1)}, f32[32768]{0:T(1024)}, s32[4]{0:T(128)S(1)}, f32[6,18,2050]{2,1,0:T(8,128)S(1)}, /*index=5*/f32[16,...) while((s32[]{:T(128)}, f32[3,32768]{1,0:T(4,128)S(1)}, ...), condition=%wide.region_3.4_spmd.clone, body=%wide.region_0.3_spmd.clone.sunk | while | flops 105480208 | bytes 23315676 | solution.py:92
  27.1 0.9 dynamic-slice_bitcast_fusion.7
  28.7 2.1 %convolution_bitcast_fusion.2 = f32[16,32768]{1,0:T(8,128)S(1)} fusion(f32[16,16]{1,0:T(8,128)S(1)} %get-tuple-element.308, f32[32768]{0:T(1024)S(1)} %bitcast.78), kind=kOutput, calls=%fused_computation.1.clone.1 | convolution fusion | flops 102760448 | bytes 2229248 | tf_op jit(solution)/shard_map/while/body/eval_jaxpr/dot_general | solution.py:38
  31.3 2.1 %reshape.152 = f32[4,3,32768]{2,1,0:T(4,128)} reshape(f32[12,32768]{1,0:T(8,128)S(1)} %bitcast.70) | data formatting | bytes 3145728 | tf_op jit(solution)/shard_map/while/body/eval_jaxpr/reshape | solution.py:48
  33.4 2.4 %multiply_reduce_fusion.2 = f32[3,32768]{1,0:T(4,128)S(1)} fusion(f32[4,3,32768]{2,1,0:T(4,128)} %reshape.152, f32[4,32768]{1,0:T(4,128)S(1)} %fusion.35), kind=kLoop, calls=%fused_computation.2.clone.1 | loop fusion | flops 688128 | bytes 2490368 | tf_op jit(solution)/shard_map/while/body/eval_jaxpr/reduce_sum | solution.py:47
  42.9 0.9 dynamic-slice_bitcast_fusion.7
  44.5 2.1 %convolution_bitcast_fusion.2 = f32[16,32768]{1,0:T(8,128)S(1)} fusion(f32[16,16]{1,0:T(8,128)S(1)} %get-tuple-element.308, f32[32768]{0:T(1024)S(1)} %bitcast.78), kind=kOutput, calls=%fused_computation.1.clone.1 | convolution fusion | flops 102760448 | bytes 2229248 | tf_op jit(solution)/shard_map/while/body/eval_jaxpr/dot_general | solution.py:38
  47.1 2.1 %reshape.152 = f32[4,3,32768]{2,1,0:T(4,128)} reshape(f32[12,32768]{1,0:T(8,128)S(1)} %bitcast.70) | data formatting | bytes 3145728 | tf_op jit(solution)/shard_map/while/body/eval_jaxpr/reshape | solution.py:48
  49.1 2.4 %multiply_reduce_fusion.2 = f32[3,32768]{1,0:T(4,128)S(1)} fusion(f32[4,3,32768]{2,1,0:T(4,128)} %reshape.152, f32[4,32768]{1,0:T(4,128)S(1)} %fusion.35), kind=kLoop, calls=%fused_computation.2.clone.1 | loop fusion | flops 688128 | bytes 2490368 | tf_op jit(solution)/shard_map/while/body/eval_jaxpr/reduce_sum | solution.py:47
  58.7 0.9 dynamic-slice_bitcast_fusion.7
  60.2 2.1 %convolution_bitcast_fusion.2 = f32[16,32768]{1,0:T(8,128)S(1)} fusion(f32[16,16]{1,0:T(8,128)S(1)} %get-tuple-element.308, f32[32768]{0:T(1024)S(1)} %bitcast.78), kind=kOutput, calls=%fused_computation.1.clone.1 | convolution fusion | flops 102760448 | bytes 2229248 | tf_op jit(solution)/shard_map/while/body/eval_jaxpr/dot_general | solution.py:38
  62.8 2.1 %reshape.152 = f32[4,3,32768]{2,1,0:T(4,128)} reshape(f32[12,32768]{1,0:T(8,128)S(1)} %bitcast.70) | data formatting | bytes 3145728 | tf_op jit(solution)/shard_map/while/body/eval_jaxpr/reshape | solution.py:48
  64.9 2.4 %multiply_reduce_fusion.2 = f32[3,32768]{1,0:T(4,128)S(1)} fusion(f32[4,3,32768]{2,1,0:T(4,128)} %reshape.152, f32[4,32768]{1,0:T(4,128)S(1)} %fusion.35), kind=kLoop, calls=%fused_computation.2.clone.1 | loop fusion | flops 688128 | bytes 2490368 | tf_op jit(solution)/shard_map/while/body/eval_jaxpr/reduce_sum | solution.py:47
  74.4 0.9 dynamic-slice_bitcast_fusion.7
  76.0 2.1 %convolution_bitcast_fusion.2 = f32[16,32768]{1,0:T(8,128)S(1)} fusion(f32[16,16]{1,0:T(8,128)S(1)} %get-tuple-element.308, f32[32768]{0:T(1024)S(1)} %bitcast.78), kind=kOutput, calls=%fused_computation.1.clone.1 | convolution fusion | flops 102760448 | bytes 2229248 | tf_op jit(solution)/shard_map/while/body/eval_jaxpr/dot_general | solution.py:38
  78.6 2.1 %reshape.152 = f32[4,3,32768]{2,1,0:T(4,128)} reshape(f32[12,32768]{1,0:T(8,128)S(1)} %bitcast.70) | data formatting | bytes 3145728 | tf_op jit(solution)/shard_map/while/body/eval_jaxpr/reshape | solution.py:48
  80.6 2.4 %multiply_reduce_fusion.2 = f32[3,32768]{1,0:T(4,128)S(1)} fusion(f32[4,3,32768]{2,1,0:T(4,128)} %reshape.152, f32[4,32768]{1,0:T(4,128)S(1)} %fusion.35), kind=kLoop, calls=%fused_computation.2.clone.1 | loop fusion | flops 688128 | bytes 2490368 | tf_op jit(solution)/shard_map/while/body/eval_jaxpr/reduce_sum | solution.py:47
  84.4 0.9 concatenate.35
  85.7 3.1 %copy.11 = f32[4,16,2048]{1,0,2:T(4,128)} copy(f32[4,16,2048]{2,1,0:T(8,128)S(1)} %pad_maximum_fusion) | data formatting | bytes 1048576 | tf_op jit(solution)/shard_map/concatenate | solution.py:93
  88.7 4.8 %reshape.149 = f32[32,1,4096]{2,1,0:T(1,128)S(1)} reshape(f32[2048,4,16]{2,1,0:T(4,128)} %bitcast.75) | data formatting | bytes 1048576
  93.5 23.0 %all_to_all.15 = f32[32,1,4096]{2,1,0:T(1,128)S(1)} all-to-all(f32[32,1,4096]{2,1,0:T(1,128)S(1)} %reshape.149), channel_id=1, replica_groups=mesh['depth'=32,'strip'=16] {'depth'}, dimensions={0} | all-to-all | bytes 1048576 | tf_op jit(solution)/shard_map/all_to_all | solution.py:99
  117.0 1.9 %reduce = f32[32,4096]{1,0:T(8,128)S(1)} reduce(f32[32,1,4096]{2,1,0:T(1,128)S(1)} %all_to_all.15, f32[]{:T(128)} %broadcast.229), dimensions={1}, to_apply=%all_to_all.11.reduce_sub_computation | reduce | bytes 1048580 | tf_op jit(solution)/shard_map/all_to_all | solution.py:99
  118.9 4.3 %reshape.150 = f32[2048,4,16]{2,1,0:T(4,128)} reshape(f32[32,4096]{1,0:T(8,128)S(1)} %reduce) | data formatting | bytes 1048576
  123.2 3.5 %copy.13 = f32[4,16,32,64]{3,2,1,0:T(8,128)S(1)} copy(f32[4,16,32,64]{1,0,3,2:T(4,128)} %bitcast.74) | data formatting | bytes 1048576 | tf_op jit(solution)/shard_map/all_to_all | solution.py:99
  (137 shorter events, 17.4 us)
Async XLA Ops:
  0.0 16.5 %copy-start.4 = (f32[4,16]{1,0:T(4,128)S(1)}, f32[4,16]{1,0:T(4,128)}, u32[]{:S(2)}) copy-start(f32[4,16]{1,0:T(4,128)} %param.11) | copy-start | bytes 772
  1.0 8.7 %collective-permute-start.1 = (f32[1,16,2048]{2,1,0:T(8,128)S(1)}, f32[1,16,2048]{2,1,0:T(8,128)S(1)}, u32[]{:S(2)}, u32[]{:S(2)}) collective-permute-start(f32[1,16,2048]{2,1,0:T(8,128)S(1)} %get-tuple-element.198), channel_id=1, source_target_pairs={{16,0},{32,16},{48,32},{64,48},{80,64},{96,80},{112,96},{128,112},... | collective-permute-start | bytes 393224 | tf_op jit(solution)/shard_map/ppermute | solution.py:21
  3.6 5.0 %collective-permute-start = (f32[1,16,2048]{2,1,0:T(8,128)S(1)}, f32[1,16,2048]{2,1,0:T(8,128)S(1)}, u32[]{:S(2)}, u32[]{:S(2)}) collective-permute-start(f32[1,16,2048]{2,1,0:T(8,128)S(1)} %get-tuple-element.199), channel_id=1, source_target_pairs={{0,16},{16,32},{32,48},{48,64},{64,80},{80,96},{96,112},{112,128},... | collective-permute-start | bytes 393224 | tf_op jit(solution)/shard_map/ppermute | solution.py:20
  9.8 6.7 %collective-permute-start.2 = (f32[6,1,2048]{2,1,0:T(1,128)S(1)}, f32[6,1,2048]{2,1,0:T(1,128)S(1)}, u32[]{:S(2)}, u32[]{:S(2)}) collective-permute-start(f32[6,1,2048]{2,1,0:T(1,128)S(1)} %get-tuple-element.194), channel_id=1, source_target_pairs={{0,1},{1,2},{2,3},{3,4},{4,5},{5,6},{6,7},{7,8},{8,9},{9,10},{10,1... | collective-permute-start | bytes 147464 | tf_op jit(solution)/shard_map/ppermute | solution.py:20
  14.6 6.1 %collective-permute-start.3 = (f32[6,1,2048]{2,1,0:T(1,128)S(1)}, f32[6,1,2048]{2,1,0:T(1,128)S(1)}, u32[]{:S(2)}, u32[]{:S(2)}) collective-permute-start(f32[6,1,2048]{2,1,0:T(1,128)S(1)} %get-tuple-element.195), channel_id=1, source_target_pairs={{1,0},{2,1},{3,2},{4,3},{5,4},{6,5},{7,6},{8,7},{9,8},{10,9},{11,1... | collective-permute-start | bytes 147464 | tf_op jit(solution)/shard_map/ppermute | solution.py:21
  21.4 6.8 %copy-start.5 = (s32[4]{0:T(128)}, s32[4]{0:T(128)S(1)}, u32[]{:S(2)}) copy-start(s32[4]{0:T(128)S(1)} %get-tuple-element.306) | copy-start | bytes 52 | tf_op jit(solution)/shard_map/while
  21.4 7.3 %copy-start = (f32[6,18,2050]{2,1,0:T(8,128)}, f32[6,18,2050]{2,1,0:T(8,128)S(1)}, u32[]{:S(2)}) copy-start(f32[6,18,2050]{2,1,0:T(8,128)S(1)} %get-tuple-element.307) | copy-start | bytes 2656804 | tf_op jit(solution)/shard_map/while
  33.4 2.5 %copy-start.2 = (f32[32768]{0:T(1024)S(1)}, f32[32768]{0:T(1024)}, u32[]{:S(2)}) copy-start(f32[32768]{0:T(1024)} %get-tuple-element.290) | copy-start | bytes 393220 | tf_op jit(solution)/shard_map/while
  35.8 1.3 %copy-start.1 = (f32[6,18,2050]{2,1,0:T(8,128)S(1)}, f32[6,18,2050]{2,1,0:T(8,128)}, u32[]{:S(2)}) copy-start(f32[6,18,2050]{2,1,0:T(8,128)} %copy-done) | copy-start | bytes 2656804 | tf_op jit(solution)/shard_map/while
  35.8 1.3 %copy-start.6 = (s32[4]{0:T(128)S(1)}, s32[4]{0:T(128)}, u32[]{:S(2)}) copy-start(s32[4]{0:T(128)} %copy-done.5) | copy-start | bytes 52 | tf_op jit(solution)/shard_map/while
  35.9 0.7 copy-start.3
  37.2 6.7 %copy-start.5 = (s32[4]{0:T(128)}, s32[4]{0:T(128)S(1)}, u32[]{:S(2)}) copy-start(s32[4]{0:T(128)S(1)} %get-tuple-element.306) | copy-start | bytes 52 | tf_op jit(solution)/shard_map/while
  37.2 7.3 %copy-start = (f32[6,18,2050]{2,1,0:T(8,128)}, f32[6,18,2050]{2,1,0:T(8,128)S(1)}, u32[]{:S(2)}) copy-start(f32[6,18,2050]{2,1,0:T(8,128)S(1)} %get-tuple-element.307) | copy-start | bytes 2656804 | tf_op jit(solution)/shard_map/while
  49.1 2.5 %copy-start.2 = (f32[32768]{0:T(1024)S(1)}, f32[32768]{0:T(1024)}, u32[]{:S(2)}) copy-start(f32[32768]{0:T(1024)} %get-tuple-element.290) | copy-start | bytes 393220 | tf_op jit(solution)/shard_map/while
  51.6 1.3 %copy-start.1 = (f32[6,18,2050]{2,1,0:T(8,128)S(1)}, f32[6,18,2050]{2,1,0:T(8,128)}, u32[]{:S(2)}) copy-start(f32[6,18,2050]{2,1,0:T(8,128)} %copy-done) | copy-start | bytes 2656804 | tf_op jit(solution)/shard_map/while
  51.6 1.3 %copy-start.6 = (s32[4]{0:T(128)S(1)}, s32[4]{0:T(128)}, u32[]{:S(2)}) copy-start(s32[4]{0:T(128)} %copy-done.5) | copy-start | bytes 52 | tf_op jit(solution)/shard_map/while
  51.7 0.7 copy-start.3
  52.9 6.7 %copy-start.5 = (s32[4]{0:T(128)}, s32[4]{0:T(128)S(1)}, u32[]{:S(2)}) copy-start(s32[4]{0:T(128)S(1)} %get-tuple-element.306) | copy-start | bytes 52 | tf_op jit(solution)/shard_map/while
  52.9 7.3 %copy-start = (f32[6,18,2050]{2,1,0:T(8,128)}, f32[6,18,2050]{2,1,0:T(8,128)S(1)}, u32[]{:S(2)}) copy-start(f32[6,18,2050]{2,1,0:T(8,128)S(1)} %get-tuple-element.307) | copy-start | bytes 2656804 | tf_op jit(solution)/shard_map/while
  64.9 2.5 %copy-start.2 = (f32[32768]{0:T(1024)S(1)}, f32[32768]{0:T(1024)}, u32[]{:S(2)}) copy-start(f32[32768]{0:T(1024)} %get-tuple-element.290) | copy-start | bytes 393220 | tf_op jit(solution)/shard_map/while
  67.3 1.3 %copy-start.1 = (f32[6,18,2050]{2,1,0:T(8,128)S(1)}, f32[6,18,2050]{2,1,0:T(8,128)}, u32[]{:S(2)}) copy-start(f32[6,18,2050]{2,1,0:T(8,128)} %copy-done) | copy-start | bytes 2656804 | tf_op jit(solution)/shard_map/while
  67.3 1.3 %copy-start.6 = (s32[4]{0:T(128)S(1)}, s32[4]{0:T(128)}, u32[]{:S(2)}) copy-start(s32[4]{0:T(128)} %copy-done.5) | copy-start | bytes 52 | tf_op jit(solution)/shard_map/while
  67.4 0.7 copy-start.3
  68.7 6.7 %copy-start.5 = (s32[4]{0:T(128)}, s32[4]{0:T(128)S(1)}, u32[]{:S(2)}) copy-start(s32[4]{0:T(128)S(1)} %get-tuple-element.306) | copy-start | bytes 52 | tf_op jit(solution)/shard_map/while
  68.7 7.3 %copy-start = (f32[6,18,2050]{2,1,0:T(8,128)}, f32[6,18,2050]{2,1,0:T(8,128)S(1)}, u32[]{:S(2)}) copy-start(f32[6,18,2050]{2,1,0:T(8,128)S(1)} %get-tuple-element.307) | copy-start | bytes 2656804 | tf_op jit(solution)/shard_map/while
  80.6 2.5 %copy-start.2 = (f32[32768]{0:T(1024)S(1)}, f32[32768]{0:T(1024)}, u32[]{:S(2)}) copy-start(f32[32768]{0:T(1024)} %get-tuple-element.290) | copy-start | bytes 393220 | tf_op jit(solution)/shard_map/while
  83.1 1.3 %copy-start.1 = (f32[6,18,2050]{2,1,0:T(8,128)S(1)}, f32[6,18,2050]{2,1,0:T(8,128)}, u32[]{:S(2)}) copy-start(f32[6,18,2050]{2,1,0:T(8,128)} %copy-done) | copy-start | bytes 2656804 | tf_op jit(solution)/shard_map/while
  83.1 1.3 %copy-start.6 = (s32[4]{0:T(128)S(1)}, s32[4]{0:T(128)}, u32[]{:S(2)}) copy-start(s32[4]{0:T(128)} %copy-done.5) | copy-start | bytes 52 | tf_op jit(solution)/shard_map/while
  83.2 0.7 copy-start.3
where the time goes:
time: 131 us; the launch traced here: 130 us
  local copies, waits for them, and re-layouts  40.5 us (31%)
  blocking collectives  23 us (18%)
  loops' own time  20.8 us (16%)
  other arithmetic  19.3 us (15%)
  starting transfers between devices  12.4 us (9%)
  matrix products  8.57 us (7%)
  waiting for transfers between devices  4.66 us (4%)
    all_to_all x1, blocking collectives, on_device(): lax.all_to_all(partial_value, 'depth', split_axis=2, concat_axis=1, tiled...  23 us
    another operation x1, loops' own time, on_device(): lax.scan(advance, start, jnp.arange(slab_depth, dtype=jnp.int32))  20.8 us
    unnamed x8, local copies, waits for them, and re-layouts  11.1 us
    reduce_sum x4, other arithmetic, shade_slice(): jnp.sum(looked[:3 * material_count].reshape(material_count, 3, -1) * oneh...  9.79 us
    dot_general x4, matrix products, shade_slice(): jnp.dot(knot_table, tent_weights, precision=lax.Precision.HIGHEST, prefer...  8.57 us
    reshape x4, local copies, waits for them, and re-layouts, shade_slice(): looked[:3 * material_count].reshape(material_count, 3, -1)  8.23 us
    ppermute x2, starting transfers between devices, with_halo(): before = lax.ppermute(last, axis, up)  7.86 us
    while x72, local copies, waits for them, and re-layouts  7.4 us
  transfers between devices with their start and end apart: 4, of which 2 were waited for; matrix products, arithmetic and copies ran while one was open for 2% of the time, Pallas kernels for 0%

commit v1 on v0

--- a/solution.py
+++ b/solution.py
@@ -2,6 +2,7 @@
 import jax.numpy as jnp
 from jax import lax
 from jax.sharding import PartitionSpec as P
+from jax.lax import all_to_all, axis_size
 
 light_x = 1.0 / 3.0
 light_y = 2.0 / 3.0
@@ -96,7 +97,15 @@
     groups = lax.axis_size("depth")
     levels = groups.bit_length() - 1
     block_width = columns // groups
-    pieces = lax.all_to_all(partial_value, "depth", split_axis=2, concat_axis=1, tiled=True)
+    pieces = jnp.concatenate(
+        all_to_all(
+            jnp.stack(jnp.split(partial_value, axis_size("depth"), axis=2)),
+            axis_name="depth",
+            split_axis=0,
+            concat_axis=0,
+        ),
+        axis=1,
+    )
     pieces = pieces.reshape(4, groups, row_count, block_width)
     for section_bit in range(levels):
         pieces = composite_over(pieces[:, 0::2], pieces[:, 1::2])

time: 131 us -> 121 us (0.924)
  local copies, waits for them, and re-layouts: 40.5 us -> 29 us
  loops' own time: 20.8 us -> 22.8 us
    unnamed x8 -> x39, local copies, waits for them, and re-layouts: 11.1 us -> 4.31 us
    all_to_all x2 -> x1, local copies, waits for them, and re-layouts: 4.06 us -> 0.51 us  [on_device(): all_to_all(jnp.stack(jnp.split(partial_value, axis_size('depth'), axis=2)...]
    concatenate x2, local copies, waits for them, and re-layouts: 4 us -> 0.94 us  [on_device(): jnp.concatenate([radiance, transmit[None, :]], axis=0)]
    dynamic_slice x4, local copies, waits for them, and re-layouts: 2.69 us -> 5.29 us  [on_device(): lax.scan(advance, start, jnp.arange(slab_depth, dtype=jnp.int32))]
    another operation x1, loops' own time: 20.8 us -> 22.8 us  [on_device(): lax.scan(advance, start, jnp.arange(slab_depth, dtype=jnp.int32))]
    slice x8 -> x4, local copies, waits for them, and re-layouts: 1.65 us -> 0.16 us  [on_device(): pieces = composite_over(pieces[:, 0::2], pieces[:, 1::2])]
    while x72 -> x56, local copies, waits for them, and re-layouts: 7.4 us -> 7.41 us
where the time goes in v1:
time: 121 us; the launch traced here: 120 us
  local copies, waits for them, and re-layouts  29 us (24%)
  blocking collectives  23 us (19%)
  loops' own time  22.8 us (19%)
  other arithmetic  19.2 us (16%)
  starting transfers between devices  12.4 us (10%)
  matrix products  8.57 us (7%)
  waiting for transfers between devices  4.66 us (4%)
    all_to_all x1, blocking collectives, on_device(): all_to_all(jnp.stack(jnp.split(partial_value, axis_size('depth'), axis=2)...  23 us
    another operation x1, loops' own time, on_device(): lax.scan(advance, start, jnp.arange(slab_depth, dtype=jnp.int32))  22.8 us
    reduce_sum x4, other arithmetic, shade_slice(): jnp.sum(looked[:3 * material_count].reshape(material_count, 3, -1) * oneh...  9.79 us
    dot_general x4, matrix products, shade_slice(): jnp.dot(knot_table, tent_weights, precision=lax.Precision.HIGHEST, prefer...  8.57 us
    reshape x4, local copies, waits for them, and re-layouts, shade_slice(): looked[:3 * material_count].reshape(material_count, 3, -1)  8.26 us
    ppermute x2, starting transfers between devices, with_halo(): before = lax.ppermute(last, axis, up)  7.86 us
    while x56, local copies, waits for them, and re-layouts  7.41 us
    dynamic_slice x4, local copies, waits for them, and re-layouts, on_device(): lax.scan(advance, start, jnp.arange(slab_depth, dtype=jnp.int32))  5.29 us
  transfers between devices with their start and end apart: 4, of which 2 were waited for; matrix products, arithmetic and copies ran while one was open for 2% of the time, Pallas kernels for 0%

profile of v1, /device:TPU:225, one launch (start us, length us, event | category | flops | bytes accessed | tf_op | source)
XLA Modules:
  0.0 119.9 jit_solution(16835143069599641008)
XLA Ops:
  0.0 1.0 fusion.30
  1.0 2.6 %collective-permute-start.1 = (f32[1,16,2048]{2,1,0:T(8,128)S(1)}, f32[1,16,2048]{2,1,0:T(8,128)S(1)}, u32[]{:S(2)}, u32[]{:S(2)}) collective-permute-start(f32[1,16,2048]{2,1,0:T(8,128)S(1)} %get-tuple-element.202), channel_id=1, source_target_pairs={{16,0},{32,16},{48,32},{64,48},{80,64},{96,80},{112,96},{128,112},... | collective-permute-start | bytes 393224 | tf_op jit(solution)/shard_map/ppermute | solution.py:22
  3.6 3.1 %collective-permute-start = (f32[1,16,2048]{2,1,0:T(8,128)S(1)}, f32[1,16,2048]{2,1,0:T(8,128)S(1)}, u32[]{:S(2)}, u32[]{:S(2)}) collective-permute-start(f32[1,16,2048]{2,1,0:T(8,128)S(1)} %get-tuple-element.203), channel_id=1, source_target_pairs={{0,16},{16,32},{32,48},{48,64},{64,80},{80,96},{96,112},{112,128},... | collective-permute-start | bytes 393224 | tf_op jit(solution)/shard_map/ppermute | solution.py:21
  7.4 0.7 copy.70
  8.6 1.1 constant_dynamic-update-slice_fusion.1
  9.8 4.8 %collective-permute-start.2 = (f32[6,1,2048]{2,1,0:T(1,128)S(1)}, f32[6,1,2048]{2,1,0:T(1,128)S(1)}, u32[]{:S(2)}, u32[]{:S(2)}) collective-permute-start(f32[6,1,2048]{2,1,0:T(1,128)S(1)} %get-tuple-element.196), channel_id=1, source_target_pairs={{0,1},{1,2},{2,3},{3,4},{4,5},{5,6},{6,7},{7,8},{8,9},{9,10},{10,1... | collective-permute-start | bytes 147464 | tf_op jit(solution)/shard_map/ppermute | solution.py:21
  14.6 1.9 %collective-permute-start.3 = (f32[6,1,2048]{2,1,0:T(1,128)S(1)}, f32[6,1,2048]{2,1,0:T(1,128)S(1)}, u32[]{:S(2)}, u32[]{:S(2)}) collective-permute-start(f32[6,1,2048]{2,1,0:T(1,128)S(1)} %get-tuple-element.197), channel_id=1, source_target_pairs={{1,0},{2,1},{3,2},{4,3},{5,4},{6,5},{7,6},{8,7},{9,8},{10,9},{11,1... | collective-permute-start | bytes 147464 | tf_op jit(solution)/shard_map/ppermute | solution.py:22
  16.6 4.2 %collective-permute-done.3 = f32[6,1,2048]{2,1,0:T(1,128)S(1)} collective-permute-done((f32[6,1,2048]{2,1,0:T(1,128)S(1)}, f32[6,1,2048]{2,1,0:T(1,128)S(1)}, u32[]{:S(2)}, u32[]{:S(2)}) %collective-permute-start.3) | collective-permute-done | bytes 49184 | tf_op jit(solution)/shard_map/ppermute | solution.py:22
  22.0 67.7 %while.16 = (s32[]{:T(128)}, f32[3,32768]{1,0:T(4,128)S(1)}, f32[32768]{0:T(1024)}, s32[4]{0:T(128)}, f32[6,18,2050]{2,1,0:T(8,128)S(1)}, /*index=5*/f32[16,16]{...) while((s32[]{:T(128)}, f32[3,32768]{1,0:T(4,128)S(1)}, ...), condition=%wide.region_3.4_spmd.clone, body=%wide.region_0.3_spmd.clone.sunk | while | flops 105480208 | bytes 23315492 | solution.py:93
  22.0 1.3 %dynamic_slice.52 = s32[1]{0:T(128)} dynamic-slice(s32[4]{0:T(128)} %get-tuple-element.314, s32[]{:T(128)S(6)} %copy.90), dynamic_slice_sizes={1} | dynamic-slice | bytes 12 | tf_op jit(solution)/shard_map/while/body/jit(dynamic_index_in_dim)/dynamic_slice | solution.py:93
  28.9 0.9 dynamic-slice_bitcast_fusion.7
  30.4 2.1 %convolution_bitcast_fusion.2 = f32[16,32768]{1,0:T(8,128)S(1)} fusion(f32[16,16]{1,0:T(8,128)S(1)} %get-tuple-element.316, f32[32768]{0:T(1024)S(1)} %bitcast.203), kind=kOutput, calls=%fused_computation.1.clone.1 | convolution fusion | flops 102760448 | bytes 2229248 | tf_op jit(solution)/shard_map/while/body/eval_jaxpr/dot_general | solution.py:39
  33.0 2.1 %reshape.154 = f32[4,3,32768]{2,1,0:T(4,128)} reshape(f32[12,32768]{1,0:T(8,128)S(1)} %bitcast.197) | data formatting | bytes 3145728 | tf_op jit(solution)/shard_map/while/body/eval_jaxpr/reshape | solution.py:49
  35.1 2.4 %multiply_reduce_fusion.2 = f32[3,32768]{1,0:T(4,128)S(1)} fusion(f32[4,3,32768]{2,1,0:T(4,128)} %reshape.154, f32[4,32768]{1,0:T(4,128)S(1)} %fusion.40), kind=kLoop, calls=%fused_computation.2.clone.1 | loop fusion | flops 688128 | bytes 2490368 | tf_op jit(solution)/shard_map/while/body/eval_jaxpr/reduce_sum | solution.py:48
  38.9 1.3 %dynamic_slice.52 = s32[1]{0:T(128)} dynamic-slice(s32[4]{0:T(128)} %get-tuple-element.314, s32[]{:T(128)S(6)} %copy.90), dynamic_slice_sizes={1} | dynamic-slice | bytes 12 | tf_op jit(solution)/shard_map/while/body/jit(dynamic_index_in_dim)/dynamic_slice | solution.py:93
  45.8 0.9 dynamic-slice_bitcast_fusion.7
  47.4 2.1 %convolution_bitcast_fusion.2 = f32[16,32768]{1,0:T(8,128)S(1)} fusion(f32[16,16]{1,0:T(8,128)S(1)} %get-tuple-element.316, f32[32768]{0:T(1024)S(1)} %bitcast.203), kind=kOutput, calls=%fused_computation.1.clone.1 | convolution fusion | flops 102760448 | bytes 2229248 | tf_op jit(solution)/shard_map/while/body/eval_jaxpr/dot_general | solution.py:39
  50.0 2.1 %reshape.154 = f32[4,3,32768]{2,1,0:T(4,128)} reshape(f32[12,32768]{1,0:T(8,128)S(1)} %bitcast.197) | data formatting | bytes 3145728 | tf_op jit(solution)/shard_map/while/body/eval_jaxpr/reshape | solution.py:49
  52.0 2.4 %multiply_reduce_fusion.2 = f32[3,32768]{1,0:T(4,128)S(1)} fusion(f32[4,3,32768]{2,1,0:T(4,128)} %reshape.154, f32[4,32768]{1,0:T(4,128)S(1)} %fusion.40), kind=kLoop, calls=%fused_computation.2.clone.1 | loop fusion | flops 688128 | bytes 2490368 | tf_op jit(solution)/shard_map/while/body/eval_jaxpr/reduce_sum | solution.py:48
  55.8 1.3 %dynamic_slice.52 = s32[1]{0:T(128)} dynamic-slice(s32[4]{0:T(128)} %get-tuple-element.314, s32[]{:T(128)S(6)} %copy.90), dynamic_slice_sizes={1} | dynamic-slice | bytes 12 | tf_op jit(solution)/shard_map/while/body/jit(dynamic_index_in_dim)/dynamic_slice | solution.py:93
  62.7 0.9 dynamic-slice_bitcast_fusion.7
  64.3 2.1 %convolution_bitcast_fusion.2 = f32[16,32768]{1,0:T(8,128)S(1)} fusion(f32[16,16]{1,0:T(8,128)S(1)} %get-tuple-element.316, f32[32768]{0:T(1024)S(1)} %bitcast.203), kind=kOutput, calls=%fused_computation.1.clone.1 | convolution fusion | flops 102760448 | bytes 2229248 | tf_op jit(solution)/shard_map/while/body/eval_jaxpr/dot_general | solution.py:39
  66.9 2.1 %reshape.154 = f32[4,3,32768]{2,1,0:T(4,128)} reshape(f32[12,32768]{1,0:T(8,128)S(1)} %bitcast.197) | data formatting | bytes 3145728 | tf_op jit(solution)/shard_map/while/body/eval_jaxpr/reshape | solution.py:49
  69.0 2.4 %multiply_reduce_fusion.2 = f32[3,32768]{1,0:T(4,128)S(1)} fusion(f32[4,3,32768]{2,1,0:T(4,128)} %reshape.154, f32[4,32768]{1,0:T(4,128)S(1)} %fusion.40), kind=kLoop, calls=%fused_computation.2.clone.1 | loop fusion | flops 688128 | bytes 2490368 | tf_op jit(solution)/shard_map/while/body/eval_jaxpr/reduce_sum | solution.py:48
  72.8 1.3 %dynamic_slice.52 = s32[1]{0:T(128)} dynamic-slice(s32[4]{0:T(128)} %get-tuple-element.314, s32[]{:T(128)S(6)} %copy.90), dynamic_slice_sizes={1} | dynamic-slice | bytes 12 | tf_op jit(solution)/shard_map/while/body/jit(dynamic_index_in_dim)/dynamic_slice | solution.py:93
  79.7 0.9 dynamic-slice_bitcast_fusion.7
  81.2 2.1 %convolution_bitcast_fusion.2 = f32[16,32768]{1,0:T(8,128)S(1)} fusion(f32[16,16]{1,0:T(8,128)S(1)} %get-tuple-element.316, f32[32768]{0:T(1024)S(1)} %bitcast.203), kind=kOutput, calls=%fused_computation.1.clone.1 | convolution fusion | flops 102760448 | bytes 2229248 | tf_op jit(solution)/shard_map/while/body/eval_jaxpr/dot_general | solution.py:39
  83.8 2.1 %reshape.154 = f32[4,3,32768]{2,1,0:T(4,128)} reshape(f32[12,32768]{1,0:T(8,128)S(1)} %bitcast.197) | data formatting | bytes 3145728 | tf_op jit(solution)/shard_map/while/body/eval_jaxpr/reshape | solution.py:49
  85.9 2.4 %multiply_reduce_fusion.2 = f32[3,32768]{1,0:T(4,128)S(1)} fusion(f32[4,3,32768]{2,1,0:T(4,128)} %reshape.154, f32[4,32768]{1,0:T(4,128)S(1)} %fusion.40), kind=kLoop, calls=%fused_computation.2.clone.1 | loop fusion | flops 688128 | bytes 2490368 | tf_op jit(solution)/shard_map/while/body/eval_jaxpr/reduce_sum | solution.py:48
  89.7 0.9 concatenate.35
  92.9 23.0 %all_to_all.5 = f32[32,1,4096]{2,1,0:T(1,128)S(1)} all-to-all(f32[32,1,4096]{2,1,0:T(1,128)S(1)} %reshape.151), channel_id=1, replica_groups=mesh['depth'=32,'strip'=16] {'depth'}, dimensions={0} | all-to-all | bytes 1048576 | tf_op jit(solution)/shard_map/all_to_all | solution.py:101
  116.4 1.9 %reduce = f32[32,4096]{1,0:T(8,128)S(1)} reduce(f32[32,1,4096]{2,1,0:T(1,128)S(1)} %all_to_all.5, f32[]{:T(128)} %broadcast.229), dimensions={1}, to_apply=%all_to_all.3.reduce_sub_computation | reduce | bytes 1048580 | tf_op jit(solution)/shard_map/all_to_all | solution.py:101
  (147 shorter events, 16.0 us)
Async XLA Ops:
  0.0 16.5 %copy-start.4 = (f32[4,16]{1,0:T(4,128)S(1)}, f32[4,16]{1,0:T(4,128)}, u32[]{:S(2)}) copy-start(f32[4,16]{1,0:T(4,128)} %param.11) | copy-start | bytes 772
  1.0 8.7 %collective-permute-start.1 = (f32[1,16,2048]{2,1,0:T(8,128)S(1)}, f32[1,16,2048]{2,1,0:T(8,128)S(1)}, u32[]{:S(2)}, u32[]{:S(2)}) collective-permute-start(f32[1,16,2048]{2,1,0:T(8,128)S(1)} %get-tuple-element.202), channel_id=1, source_target_pairs={{16,0},{32,16},{48,32},{64,48},{80,64},{96,80},{112,96},{128,112},... | collective-permute-start | bytes 393224 | tf_op jit(solution)/shard_map/ppermute | solution.py:22
  3.6 5.0 %collective-permute-start = (f32[1,16,2048]{2,1,0:T(8,128)S(1)}, f32[1,16,2048]{2,1,0:T(8,128)S(1)}, u32[]{:S(2)}, u32[]{:S(2)}) collective-permute-start(f32[1,16,2048]{2,1,0:T(8,128)S(1)} %get-tuple-element.203), channel_id=1, source_target_pairs={{0,16},{16,32},{32,48},{48,64},{64,80},{80,96},{96,112},{112,128},... | collective-permute-start | bytes 393224 | tf_op jit(solution)/shard_map/ppermute | solution.py:21
  9.8 6.7 %collective-permute-start.2 = (f32[6,1,2048]{2,1,0:T(1,128)S(1)}, f32[6,1,2048]{2,1,0:T(1,128)S(1)}, u32[]{:S(2)}, u32[]{:S(2)}) collective-permute-start(f32[6,1,2048]{2,1,0:T(1,128)S(1)} %get-tuple-element.196), channel_id=1, source_target_pairs={{0,1},{1,2},{2,3},{3,4},{4,5},{5,6},{6,7},{7,8},{8,9},{9,10},{10,1... | collective-permute-start | bytes 147464 | tf_op jit(solution)/shard_map/ppermute | solution.py:21
  14.6 6.1 %collective-permute-start.3 = (f32[6,1,2048]{2,1,0:T(1,128)S(1)}, f32[6,1,2048]{2,1,0:T(1,128)S(1)}, u32[]{:S(2)}, u32[]{:S(2)}) collective-permute-start(f32[6,1,2048]{2,1,0:T(1,128)S(1)} %get-tuple-element.197), channel_id=1, source_target_pairs={{1,0},{2,1},{3,2},{4,3},{5,4},{6,5},{7,6},{8,7},{9,8},{10,9},{11,1... | collective-permute-start | bytes 147464 | tf_op jit(solution)/shard_map/ppermute | solution.py:22
  22.0 8.4 %copy-start = (f32[6,18,2050]{2,1,0:T(8,128)}, f32[6,18,2050]{2,1,0:T(8,128)S(1)}, u32[]{:S(2)}) copy-start(f32[6,18,2050]{2,1,0:T(8,128)S(1)} %get-tuple-element.315) | copy-start | bytes 2656804 | tf_op jit(solution)/shard_map/while
  35.1 2.5 %copy-start.2 = (f32[32768]{0:T(1024)S(1)}, f32[32768]{0:T(1024)}, u32[]{:S(2)}) copy-start(f32[32768]{0:T(1024)} %get-tuple-element.298) | copy-start | bytes 393220 | tf_op jit(solution)/shard_map/while
  37.5 1.3 %copy-start.1 = (f32[6,18,2050]{2,1,0:T(8,128)S(1)}, f32[6,18,2050]{2,1,0:T(8,128)}, u32[]{:S(2)}) copy-start(f32[6,18,2050]{2,1,0:T(8,128)} %copy-done) | copy-start | bytes 2656804 | tf_op jit(solution)/shard_map/while
  37.6 0.6 copy-start.3
  38.9 8.4 %copy-start = (f32[6,18,2050]{2,1,0:T(8,128)}, f32[6,18,2050]{2,1,0:T(8,128)S(1)}, u32[]{:S(2)}) copy-start(f32[6,18,2050]{2,1,0:T(8,128)S(1)} %get-tuple-element.315) | copy-start | bytes 2656804 | tf_op jit(solution)/shard_map/while
  52.0 2.5 %copy-start.2 = (f32[32768]{0:T(1024)S(1)}, f32[32768]{0:T(1024)}, u32[]{:S(2)}) copy-start(f32[32768]{0:T(1024)} %get-tuple-element.298) | copy-start | bytes 393220 | tf_op jit(solution)/shard_map/while
  54.5 1.3 %copy-start.1 = (f32[6,18,2050]{2,1,0:T(8,128)S(1)}, f32[6,18,2050]{2,1,0:T(8,128)}, u32[]{:S(2)}) copy-start(f32[6,18,2050]{2,1,0:T(8,128)} %copy-done) | copy-start | bytes 2656804 | tf_op jit(solution)/shard_map/while
  54.6 0.6 copy-start.3
  55.8 8.4 %copy-start = (f32[6,18,2050]{2,1,0:T(8,128)}, f32[6,18,2050]{2,1,0:T(8,128)S(1)}, u32[]{:S(2)}) copy-start(f32[6,18,2050]{2,1,0:T(8,128)S(1)} %get-tuple-element.315) | copy-start | bytes 2656804 | tf_op jit(solution)/shard_map/while
  69.0 2.5 %copy-start.2 = (f32[32768]{0:T(1024)S(1)}, f32[32768]{0:T(1024)}, u32[]{:S(2)}) copy-start(f32[32768]{0:T(1024)} %get-tuple-element.298) | copy-start | bytes 393220 | tf_op jit(solution)/shard_map/while
  71.4 1.3 %copy-start.1 = (f32[6,18,2050]{2,1,0:T(8,128)S(1)}, f32[6,18,2050]{2,1,0:T(8,128)}, u32[]{:S(2)}) copy-start(f32[6,18,2050]{2,1,0:T(8,128)} %copy-done) | copy-start | bytes 2656804 | tf_op jit(solution)/shard_map/while
  71.5 0.6 copy-start.3
  72.8 8.4 %copy-start = (f32[6,18,2050]{2,1,0:T(8,128)}, f32[6,18,2050]{2,1,0:T(8,128)S(1)}, u32[]{:S(2)}) copy-start(f32[6,18,2050]{2,1,0:T(8,128)S(1)} %get-tuple-element.315) | copy-start | bytes 2656804 | tf_op jit(solution)/shard_map/while
  85.9 2.5 %copy-start.2 = (f32[32768]{0:T(1024)S(1)}, f32[32768]{0:T(1024)}, u32[]{:S(2)}) copy-start(f32[32768]{0:T(1024)} %get-tuple-element.298) | copy-start | bytes 393220 | tf_op jit(solution)/shard_map/while
  88.4 1.3 %copy-start.1 = (f32[6,18,2050]{2,1,0:T(8,128)S(1)}, f32[6,18,2050]{2,1,0:T(8,128)}, u32[]{:S(2)}) copy-start(f32[6,18,2050]{2,1,0:T(8,128)} %copy-done) | copy-start | bytes 2656804 | tf_op jit(solution)/shard_map/while
  88.4 0.6 copy-start.3
